TPU v7x, 32 devices: a whole 2x2x4 slice. The times are simulated.
32 devices in a mesh: parts: 2 (over x), col: 16 (over z, y, core).
Axes of the slice: x: 2, y: 2, z: 4, core: 2. Of those that a mesh axis runs over, the one named last changes fastest.
Arguments:
- view_factors: bfloat16 [8192, 4096], P(('parts', 'col')), parts along dimension 0, may hold values from -0.09375 to 0.09375
- direct_coeff: bfloat16 [8192, 2304], P(('parts', 'col')), parts along dimension 0, may hold values from -6 to 6
- material: int32 [8192], P(('parts', 'col')), parts along dimension 0, may hold values from 0 to 15
- albedo: float32 [32], P('parts'), parts along dimension 0, may hold values from 0.1 to 0.9
- sky_matrix: bfloat16 [2304, 128], P('col'), may hold values from -0.125 to 0.125
- sky_order: int32 [2304], replicated, may hold values from 0 to 2303, each once
Outputs:
- irradiance: bfloat16 [8192, 128], P(('parts', 'col')), parts along dimension 0
There are 2 independent parts, one for each index of `parts`. A program takes and returns all parts, laid end to end along the dimension named above; an argument that names none is the same for every part. Nothing has to cross between parts.
Inputs may be any that keep to these rules, and one draw needn't show every extreme that they name: sky_order names each of 0 to 2303 once.
All inputs are finite; a program needn't handle non-finite values.
Results may differ from a plain program's by a relative error of at most 0.0055.
Values may be sent and summed in bfloat16 or wider, within the bound.
A program may use at most 128 MiB of HBM per device.

v0:
```python
import jax
import jax.numpy as jnp
from jax import lax
from jax.sharding import PartitionSpec as P


def split_parts(values):
    upper = values.astype(jnp.bfloat16)
    lower = (values - upper.astype(jnp.float32)).astype(jnp.bfloat16)
    return (upper, lower)


def shards(view_factors, direct_coeff, material, albedo, sky_matrix, sky_order):
    inverse = jnp.argsort(sky_order)
    direct_sorted = jnp.take(direct_coeff, inverse, axis=1)
    matches = material[:, None] == jnp.arange(albedo.shape[0], dtype=jnp.int32)[None, :]
    reflectance = jnp.sum(jnp.where(matches, albedo[None, :], 0.0), axis=1)
    reflected = (reflectance[:, None] * direct_sorted.astype(jnp.float32)).astype(jnp.bfloat16)
    piece = lax.all_gather(sky_matrix, "col", axis=0, tiled=True)
    direct_hours = jnp.dot(direct_sorted, piece, preferred_element_type=jnp.float32)
    own_reflected = jnp.dot(reflected, piece, preferred_element_type=jnp.float32)
    upper, lower = split_parts(lax.all_gather(own_reflected, "col", axis=0, tiled=True))
    running = jnp.dot(view_factors, upper, preferred_element_type=jnp.float32)
    bounce_hours = running + jnp.dot(view_factors, lower, preferred_element_type=jnp.float32)
    irradiance = direct_hours + bounce_hours
    return irradiance.astype(jnp.bfloat16)


def solution(mesh):
    return jax.shard_map(
        shards,
        mesh=mesh,
        in_specs=(
            P(("parts", "col"), None),
            P(("parts", "col"), None),
            P(("parts", "col")),
            P("parts"),
            P("col", None),
            P(),
        ),
        out_specs=P(("parts", "col"), None),
        check_vma=False,
    )
```

profile of v0, /device:TPU:0, one launch (start us, length us, event | category | flops | bytes accessed | tf_op | source)
XLA Modules:
  0.0 101.5 jit_solution(16061025368571012396)
XLA Ops:
  6.5 0.0 copy-start
  6.5 0.0 all-gather.2.cloned.1.call-start
  6.5 6.6 %sort.17 = (s32[2304]{0:T(1024)}, s32[2304]{0:T(1024)S(1)}) sort(s32[2304]{0:T(1024)} %param.11, s32[2304]{0:T(1024)S(1)} %iota.8), dimensions={0}, to_apply=%region_0.0 | sort | flops 27648 | bytes 36864 | tf_op jit(solution)/shard_map/jit(argsort)/sort | solution.py:14
  13.2 26.5 %all_gather.6 = bf16[2304,128]{1,0:T(8,128)(2,1)} all-gather(bf16[144,128]{1,0:T(8,128)(2,1)} %param.10), channel_id=1, replica_groups=mesh['parts'=2,'col'=16] {'col'}, dimensions={0}, use_global_device_ids=true | all-gather | bytes 626688 | tf_op jit(solution)/shard_map/all_gather | solution.py:19
  39.7 0.0 copy-start.3
  39.7 0.0 copy-start.4
  39.7 1.6 %copy.10 = bf16[256,2304]{0,1:T(8,128)(2,1)S(1)} copy(bf16[256,2304]{1,0:T(8,128)(2,1)} %param.7) | data formatting | bytes 2359296 | tf_op args[1]
  41.3 0.0 copy-done.3
  41.3 0.0 copy-done.4
  41.3 0.1 select_reduce_fusion
  41.4 7.4 %gather_fusion = bf16[2304,256]{1,0:T(8,128)(2,1)} fusion(bf16[256,2304]{0,1:T(8,128)(2,1)S(1)} %copy.10, s32[3072]{0:T(1024)S(1)} %pad_clamp_fusion), kind=kCustom, calls=%fused_computation | custom fusion | bytes 2368512 | tf_op jit(solution)/shard_map/jit(_take)/gather | solution.py:15
  48.9 0.0 copy-start.2
  48.9 3.1 %fusion = f32[256,128]{1,0:T(8,128)} fusion(bf16[2304,128]{1,0:T(8,128)(2,1)} %all_gather.6, f32[256]{0:T(256)S(1)} %select_reduce_fusion, bf16[2304,256]{1,0:T(8,128)(2,1)} %gather_fusion, pred[2304]{0:T(1024)(128)(4,1)S(1)} %compare_and_fusion), kind=kOutput, calls=%fused_computation.3 | convolution fusion | flops 153354240 | bytes 1903872 | tf_op jit(solution)/shard_map/dot_general | solution.py:21
  51.9 0.0 all-gather.2.cloned.1.call-update
  52.0 0.0 copy-done.2
  52.0 1.9 %fusion.8 = f32[256,128]{1,0:T(8,128)S(1)} fusion(bf16[2304,128]{1,0:T(8,128)(2,1)} %all_gather.6, bf16[2304,256]{1,0:T(8,128)(2,1)S(1)} %copy-done.2, pred[2304]{0:T(1024)(128)(4,1)S(1)} %compare_and_fusion), kind=kOutput, calls=%fused_computation.13 | convolution fusion | flops 151584768 | bytes 1902848 | tf_op jit(solution)/shard_map/dot_general | solution.py:20
  53.9 36.9 %all-gather.2.cloned.1.call-done = f32[4096,128]{1,0:T(8,128)} async-done(((f32[256,128]{1,0:T(8,128)}), f32[4096,128]{1,0:T(8,128)}) %all-gather.2.cloned.1.call-update) | async-done | bytes 2097168 | tf_op jit(solution)/shard_map/all_gather | solution.py:22
  90.8 0.0 copy-done
  90.8 0.0 copy-start.1
  90.8 2.4 %fusion.6 = f32[128,256]{0,1:T(8,128)S(1)} fusion(bf16[256,4096]{1,0:T(8,128)(2,1)S(1)} %copy-done, f32[4096,128]{1,0:T(8,128)} %all-gather.2.cloned.1.call-done), kind=kOutput, calls=%fused_computation.11 | convolution fusion | flops 268959744 | bytes 4325376 | tf_op jit(solution)/shard_map/dot_general | solution.py:23
  93.3 0.0 copy-done.1
  93.3 1.3 %fusion.4 = bf16[256,128]{1,0:T(8,128)(2,1)} fusion(f32[256,128]{1,0:T(8,128)S(1)} %fusion.8, f32[128,256]{0,1:T(8,128)S(1)} %fusion.6, bf16[256,4096]{1,0:T(8,128)(2,1)S(1)} %copy-done, f32[4096,128]{1,0:T(8,128)S(1)} %copy-done.1), kind=kOutput, calls=%fused_computation.9 | convolution fusion | flops 270630912 | bytes 4521984 | tf_op jit(solution)/shard_map/dot_general | solution.py:24
  (4 shorter events, 0.0 us)
Async XLA Ops:
  6.5 84.3 %copy-start = (bf16[256,4096]{1,0:T(8,128)(2,1)S(1)}, bf16[256,4096]{1,0:T(8,128)(2,1)}, u32[]{:S(2)}) copy-start(bf16[256,4096]{1,0:T(8,128)(2,1)} %param.6) | copy-start | bytes 6291460
  6.5 84.3 %all-gather.2.cloned.1.call-start = ((), (), s32[]{:S(2)}) async-start(), calls=%async_computation | async-start | bytes 2228224 | tf_op jit(solution)/shard_map/all_gather | solution.py:22
  39.7 1.6 %copy-start.3 = (s32[256]{0:T(256)S(1)}, s32[256]{0:T(256)}, u32[]{:S(2)}) copy-start(s32[256]{0:T(256)} %param.8) | copy-start | bytes 3076
  39.7 1.6 %copy-start.4 = (f32[16]{0:T(128)S(1)}, f32[16]{0:T(128)}, u32[]{:S(2)}) copy-start(f32[16]{0:T(128)} %param.9) | copy-start | bytes 196
  48.9 3.1 %copy-start.2 = (bf16[2304,256]{1,0:T(8,128)(2,1)S(1)}, bf16[2304,256]{1,0:T(8,128)(2,1)}, u32[]{:S(2)}) copy-start(bf16[2304,256]{1,0:T(8,128)(2,1)} %gather_fusion) | copy-start | bytes 3538948
  90.8 2.4 %copy-start.1 = (f32[4096,128]{1,0:T(8,128)S(1)}, f32[4096,128]{1,0:T(8,128)}, u32[]{:S(2)}) copy-start(f32[4096,128]{1,0:T(8,128)} %all-gather.2.cloned.1.call-done) | copy-start | bytes 6291460
Sparse Core Ops, SparseCore 0:
  52.1 38.6 all-gather.1
where the time goes:
time: 102 us; the launch traced here: 101 us
  waiting for transfers between devices  36.9 us (36%)
  blocking collectives  26.5 us (26%)
  between operations  13.5 us (13%)
  local copies, waits for them, and re-layouts  9.05 us (9%)
  matrix products  8.78 us (9%)
  other arithmetic  6.73 us (7%)
    all_gather x1, waiting for transfers between devices, shards(): lax.all_gather(own_reflected, 'col', axis=0, tiled=True)  36.9 us
    all_gather x1, blocking collectives, shards(): piece = lax.all_gather(sky_matrix, 'col', axis=0, tiled=True)  26.5 us
    gather x1, local copies, waits for them, and re-layouts, shards(): direct_sorted = jnp.take(direct_coeff, inverse, axis=1)  7.43 us
    sort x1, other arithmetic, shards(): inverse = jnp.argsort(sky_order)  6.62 us
    dot_general x1, matrix products, shards(): jnp.dot(reflected, piece, preferred_element_type=jnp.float32)  3.06 us
    dot_general x1, matrix products, shards(): running = jnp.dot(view_factors, upper, preferred_element_type=jnp.float32)  2.44 us
  transfers between devices with their start and end apart: 1, of which 1 were waited for; matrix products, arithmetic and copies ran while one was open for 2% of the time, Pallas kernels for 0%

commit v1 on v0

--- a/solution.py
+++ b/solution.py
@@ -2,6 +2,28 @@
 import jax.numpy as jnp
 from jax import lax
 from jax.sharding import PartitionSpec as P
+
+
+def joined_along(blocks, dim):
+    blocks = jnp.moveaxis(blocks, 0, dim)
+    lengths = blocks.shape
+    return blocks.reshape(*lengths[:dim], lengths[dim] * lengths[dim + 1], *lengths[dim + 2 :])
+
+
+def doubled(array, axis):
+    peers = lax.axis_size(axis)
+    tiles = array[None]
+    for level in range(peers.bit_length() - 1):
+        bit = 1 << level
+        other = lax.ppermute(tiles, axis, [(i, i ^ bit) for i in range(peers)])
+        both = jnp.stack([tiles, other])
+        upper = lax.axis_index(axis) >> level & 1
+        tiles = jnp.where(upper == 0, both, both[::-1]).reshape(-1, *array.shape)
+    return tiles
+
+
+def gather_by_bits(array, axis, dim):
+    return joined_along(doubled(array, axis), dim)
 
 
 def split_parts(values):
@@ -19,7 +41,7 @@
     piece = lax.all_gather(sky_matrix, "col", axis=0, tiled=True)
     direct_hours = jnp.dot(direct_sorted, piece, preferred_element_type=jnp.float32)
     own_reflected = jnp.dot(reflected, piece, preferred_element_type=jnp.float32)
-    upper, lower = split_parts(lax.all_gather(own_reflected, "col", axis=0, tiled=True))
+    upper, lower = split_parts(gather_by_bits(own_reflected, "col", 0))
     running = jnp.dot(view_factors, upper, preferred_element_type=jnp.float32)
     bounce_hours = running + jnp.dot(view_factors, lower, preferred_element_type=jnp.float32)
     irradiance = direct_hours + bounce_hours

time: 102 us -> 120 us (1.18)
  waiting for transfers between devices: 36.9 us -> 67.7 us
  between operations: 13.5 us -> 0.18 us
  other arithmetic: 6.73 us -> 8.83 us
  matrix products: 8.78 us -> 6.69 us
    ppermute x0 -> x4, waiting for transfers between devices: none -> 67.7 us  [doubled(): other = lax.ppermute(tiles, axis, [(i, i ^ bit) for i in range(peers)])]
    all_gather x1 -> x0, waiting for transfers between devices: 36.9 us -> none  [shards(): lax.all_gather(own_reflected, 'col', axis=0, tiled=True)]
    another operation x0 -> x5, other arithmetic: none -> 1.53 us  [doubled(): both = jnp.stack([tiles, other])]
  transfers between devices with their start and end apart: 1 -> 4, of which waited for: 1 -> 4; matrix products, arithmetic and copies ran while one was open for 2% -> 2% of each run, Pallas kernels for 0% -> 0%
where the time goes in v1:
time: 120 us
  waiting for transfers between devices  67.7 us (56%)
  blocking collectives  26.5 us (22%)
  local copies, waits for them, and re-layouts  9.01 us (8%)
  other arithmetic  8.83 us (7%)
  matrix products  6.69 us (6%)
    ppermute x4, waiting for transfers between devices, doubled(): other = lax.ppermute(tiles, axis, [(i, i ^ bit) for i in range(peers)])  67.7 us
    all_gather x1, blocking collectives, shards(): piece = lax.all_gather(sky_matrix, 'col', axis=0, tiled=True)  26.5 us
    gather x1, local copies, waits for them, and re-layouts, shards(): direct_sorted = jnp.take(direct_coeff, inverse, axis=1)  7.43 us
    sort x1, other arithmetic, shards(): inverse = jnp.argsort(sky_order)  6.62 us
  transfers between devices with their start and end apart: 4, of which 4 were waited for; matrix products, arithmetic and copies ran while one was open for 2% of the time, Pallas kernels for 0%

profile of v1, /device:TPU:0, one launch (start us, length us, event | category | flops | bytes accessed | tf_op | source)
XLA Modules:
  0.0 119.6 jit_solution(1579036148831763194)
XLA Ops:
  0.0 0.0 copy-start
  0.0 0.0 copy-start.2
  0.0 0.0 copy-start.1
  0.0 6.6 %sort.17 = (s32[2304]{0:T(1024)}, s32[2304]{0:T(1024)S(1)}) sort(s32[2304]{0:T(1024)} %param.11, s32[2304]{0:T(1024)S(1)} %iota.8), dimensions={0}, to_apply=%region_0.0 | sort | flops 27648 | bytes 36864 | tf_op jit(solution)/shard_map/jit(argsort)/sort | solution.py:36
  6.7 26.5 %all_gather.3 = bf16[2304,128]{1,0:T(8,128)(2,1)} all-gather(bf16[144,128]{1,0:T(8,128)(2,1)} %param.10), channel_id=1, replica_groups=mesh['parts'=2,'col'=16] {'col'}, dimensions={0}, use_global_device_ids=true | all-gather | bytes 626688 | tf_op jit(solution)/shard_map/all_gather | solution.py:41
  33.2 1.6 %copy.10 = bf16[256,2304]{0,1:T(8,128)(2,1)S(1)} copy(bf16[256,2304]{1,0:T(8,128)(2,1)} %param.7) | data formatting | bytes 2359296 | tf_op args[1]
  34.8 0.0 copy-done.2
  34.8 0.0 copy-done.1
  34.8 0.1 select_reduce_fusion
  34.9 7.4 %gather_fusion = bf16[2304,256]{1,0:T(8,128)(2,1)} fusion(bf16[256,2304]{0,1:T(8,128)(2,1)S(1)} %copy.10, s32[3072]{0:T(1024)S(1)} %pad_clamp_fusion), kind=kCustom, calls=%fused_computation | custom fusion | bytes 2368512 | tf_op jit(solution)/shard_map/jit(_take)/gather | solution.py:37
  42.3 2.3 %fusion.1 = f32[256,128]{1,0:T(8,128)S(1)} fusion(bf16[2304,128]{1,0:T(8,128)(2,1)} %all_gather.3, f32[256]{0:T(256)S(1)} %select_reduce_fusion, bf16[2304,256]{1,0:T(8,128)(2,1)} %gather_fusion, pred[2304]{0:T(1024)(128)(4,1)S(1)} %compare_and_fusion), kind=kOutput, calls=%fused_computation.8 | convolution fusion | flops 153354240 | bytes 1903872 | tf_op jit(solution)/shard_map/dot_general | solution.py:43
  44.6 0.4 collective-permute-start
  45.1 1.0 collective-permute-done
  46.1 0.1 collective-permute-start.1
  46.2 8.5 %collective-permute-done.1 = f32[2,256,128]{2,1,0:T(8,128)S(1)} collective-permute-done((f32[2,256,128]{2,1,0:T(8,128)S(1)}, f32[2,256,128]{2,1,0:T(8,128)S(1)}, u32[]{:S(2)}, u32[]{:S(2)}) %collective-permute-start.1) | collective-permute-done | bytes 262176 | tf_op jit(solution)/shard_map/ppermute | solution.py:18
  54.8 0.1 collective-permute-start.2
  54.9 13.3 %collective-permute-done.2 = f32[4,256,128]{2,1,0:T(8,128)S(1)} collective-permute-done((f32[4,256,128]{2,1,0:T(8,128)S(1)}, f32[4,256,128]{2,1,0:T(8,128)S(1)}, u32[]{:S(2)}, u32[]{:S(2)}) %collective-permute-start.2) | collective-permute-done | bytes 524320 | tf_op jit(solution)/shard_map/ppermute | solution.py:18
  68.2 0.1 pad_maximum_fusion.1
  68.3 0.1 reverse_select_fusion.1
  68.4 0.1 collective-permute-start.3
  68.5 2.3 %fusion.6 = f32[256,128]{1,0:T(8,128)S(1)} fusion(bf16[2304,128]{1,0:T(8,128)(2,1)} %all_gather.3, bf16[2304,256]{1,0:T(8,128)(2,1)} %gather_fusion, pred[2304]{0:T(1024)(128)(4,1)S(1)} %compare_and_fusion), kind=kOutput, calls=%fused_computation.18 | convolution fusion | flops 151584768 | bytes 1902848 | tf_op jit(solution)/shard_map/dot_general | solution.py:42
  70.8 44.8 %collective-permute-done.3 = f32[8,256,128]{2,1,0:T(8,128)} collective-permute-done((f32[8,256,128]{2,1,0:T(8,128)S(1)}, f32[8,256,128]{2,1,0:T(8,128)}, u32[]{:S(2)}, u32[]{:S(2)}) %collective-permute-start.3) | collective-permute-done | bytes 1048608 | tf_op jit(solution)/shard_map/ppermute | solution.py:18
  115.6 1.4 %pad_maximum_fusion = f32[2,8,256,128]{3,2,1,0:T(8,128)S(1)} fusion(f32[1,8,256,128]{3,2,1,0:T(8,128)} %bitcast.11, f32[1,8,256,128]{3,2,1,0:T(8,128)S(1)} %bitcast.33), kind=kLoop, calls=%fused_computation.3 | loop fusion | flops 524288 | bytes 4194304 | tf_op jit(solution)/shard_map/stack | solution.py:19
  117.0 0.2 reverse_select_fusion
  117.2 0.3 fusion
  117.5 0.0 copy-done
  117.5 0.7 fusion.11
  118.2 1.4 %fusion.5 = bf16[256,128]{1,0:T(8,128)(2,1)} fusion(f32[256,128]{1,0:T(8,128)S(1)} %fusion.6, f32[128,256]{0,1:T(8,128)S(1)} %fusion.11, bf16[256,4096]{1,0:T(8,128)(2,1)S(1)} %copy-done, bf16[4096,128]{1,0:T(8,128)(2,1)S(1)} %get-tuple-element.8), kind=kOutput, calls=%fused_computation.14 | convolution fusion | flops 268533760 | bytes 3473408 | tf_op jit(solution)/shard_map/dot_general | solution.py:45
  (8 shorter events, 0.2 us)
Async XLA Ops:
  0.0 117.5 %copy-start = (bf16[256,4096]{1,0:T(8,128)(2,1)S(1)}, bf16[256,4096]{1,0:T(8,128)(2,1)}, u32[]{:S(2)}) copy-start(bf16[256,4096]{1,0:T(8,128)(2,1)} %param.6) | copy-start | bytes 6291460
  0.0 34.8 %copy-start.2 = (f32[16]{0:T(128)S(1)}, f32[16]{0:T(128)}, u32[]{:S(2)}) copy-start(f32[16]{0:T(128)} %param.9) | copy-start | bytes 196
  0.0 34.8 %copy-start.1 = (s32[256]{0:T(256)S(1)}, s32[256]{0:T(256)}, u32[]{:S(2)}) copy-start(s32[256]{0:T(256)} %param.8) | copy-start | bytes 3076
  44.6 1.4 %collective-permute-start = (f32[1,256,128]{2,1,0:T(8,128)S(1)}, f32[1,256,128]{2,1,0:T(8,128)S(1)}, u32[]{:S(2)}, u32[]{:S(2)}) collective-permute-start(f32[1,256,128]{2,1,0:T(8,128)S(1)} %bitcast.38), channel_id=1, source_target_pairs={{0,1},{1,0},{2,3},{3,2},{4,5},{5,4},{6,7},{7,6},{8,9},{9,8},{10,11... | collective-permute-start | bytes 393224 | tf_op jit(solution)/shard_map/ppermute | solution.py:18
  46.1 8.6 %collective-permute-start.1 = (f32[2,256,128]{2,1,0:T(8,128)S(1)}, f32[2,256,128]{2,1,0:T(8,128)S(1)}, u32[]{:S(2)}, u32[]{:S(2)}) collective-permute-start(f32[2,256,128]{2,1,0:T(8,128)S(1)} %get-tuple-element.10), channel_id=1, source_target_pairs={{0,2},{1,3},{2,0},{3,1},{4,6},{5,7},{6,4},{7,5},{8,10},{9,11},{10,... | collective-permute-start | bytes 786440 | tf_op jit(solution)/shard_map/ppermute | solution.py:18
  54.8 13.4 %collective-permute-start.2 = (f32[4,256,128]{2,1,0:T(8,128)S(1)}, f32[4,256,128]{2,1,0:T(8,128)S(1)}, u32[]{:S(2)}, u32[]{:S(2)}) collective-permute-start(f32[4,256,128]{2,1,0:T(8,128)S(1)} %bitcast.34), channel_id=1, source_target_pairs={{0,4},{1,5},{2,6},{3,7},{4,0},{5,1},{6,2},{7,3},{8,12},{9,13},{10,... | collective-permute-start | bytes 1572872 | tf_op jit(solution)/shard_map/ppermute | solution.py:18
  68.4 47.2 %collective-permute-start.3 = (f32[8,256,128]{2,1,0:T(8,128)S(1)}, f32[8,256,128]{2,1,0:T(8,128)}, u32[]{:S(2)}, u32[]{:S(2)}) collective-permute-start(f32[8,256,128]{2,1,0:T(8,128)S(1)} %bitcast.32), channel_id=1, source_target_pairs={{0,8},{1,9},{2,10},{3,11},{4,12},{5,13},{6,14},{7,15},{8,0},{9,1},... | collective-permute-start | bytes 3145736 | tf_op jit(solution)/shard_map/ppermute | solution.py:18
